TPU v7x, 32 devices: a whole 2x2x4 slice. The times are simulated.
32 devices in a mesh: sub: 8 (over y, x, core), rep: 4 (over z).
Axes of the slice: x: 2, y: 2, z: 4, core: 2. Of those that a mesh axis runs over, the one named last changes fastest.
Arguments:
- loads: bfloat16 [64, 256, 1024], P('sub', 'rep'), may hold values from -6 to 6
- operators: bfloat16 [64, 1024, 1024], P('sub'), may hold values from -0.1875 to 0.1875
- owner: int32 [512, 1], P('sub'), may hold values from 0 to 7; in each aligned block of 64 rows (0 to 63, 64 to 127, ...) at most 16 rows name the same one
- dual_block: int32 [512], P('sub'), may hold values from 0 to 15
- scale_index: int32 [16384], P('sub'), may hold values from 0 to 3
- basis: bfloat16 [16384, 1024], P('sub'), may hold values from -0.046875 to 0.046875
- coarse: bfloat16 [1024, 1024], replicated, may hold values from -0.75 to 0.75
Outputs:
- start: float32 [256, 16384], P('rep', 'sub')
- resid: float32 [256, 16384], P('rep', 'sub')
Inputs may be any that keep to these rules, and one draw needn't show every extreme that they name: Among the blocks of the subdomains of one index of sub (aligned blocks of 64 rows), no owner is named more than 16 times, a bound that some block reaches.
All inputs are finite; a program needn't handle non-finite values.
Results may differ from a plain program's by a relative error of at most 0.0075.
Values may be sent and summed in bfloat16 or wider, within the bound.
A program may use at most 128 MiB of HBM per device.

v0:
```python
import functools

import jax
import jax.numpy as jnp
from jax import lax
from jax.experimental import pallas as pl
from jax.experimental.pallas import tpu as pltpu
from jax.sharding import PartitionSpec as P

BLK = 128
FLOWS = 4
MESH = pl.DeviceIdType.MESH
VMEM_LIMIT = 62 * 1024 * 1024
F32 = jnp.float32
BF16 = jnp.bfloat16


def flip(me, r, bits):
    out = me
    for b in range(bits):
        if (r >> b) & 1:
            out = out + (1 - 2 * (me // (1 << b) % 2)) * (1 << b)
    return out


def plan(bits, flows):
    rest = list(range(1, bits))
    return [[0] + (rest if f % 2 == 0 else rest[::-1]) for f in range(flows)]


def step_of(r, order):
    for t, b in enumerate(order):
        if (r >> b) & 1:
            return t
    return len(order)


def slot_table(n, order):
    table, done = {}, 0
    for t, b in enumerate(order):
        done |= 1 << b
        for r in range(n):
            if r & done == 0:
                table[(t, r)] = len(table)
    return table


def reduce_scatter(n, bits, me, local, stage, recv, send_sem, recv_sem):
    orders = plan(bits, FLOWS)
    tables = [slot_table(n, order) for order in orders]
    sends = []

    def copy_of(f, slot, src, b):
        return pltpu.make_async_remote_copy(
            src_ref=src,
            dst_ref=recv.at[f, slot],
            send_sem=send_sem.at[f, slot],
            recv_sem=recv_sem.at[f, slot],
            device_id={"sub": flip(me, 1 << b, bits)},
            device_id_type=MESH,
        )

    def total(f, r, steps):
        part = local(f, flip(me, r, bits))
        for t in range(steps):
            slot = tables[f][(t, r)]
            copy_of(f, slot, recv.at[f, slot], orders[f][t]).wait_recv()
            part = part + recv[f, slot].astype(F32)
        return part

    for t in range(bits):
        group = []
        for f in range(FLOWS):
            for r in range(n):
                if step_of(r, orders[f]) == t:
                    land = r ^ (1 << orders[f][t])
                    group.append((step_of(land, orders[f]), f, r, land))
        for _, f, r, land in sorted(group):
            stage[f, r - 1] = total(f, r, t).astype(BF16)
            copy = copy_of(f, tables[f][(t, land)], stage.at[f, r - 1], orders[f][t])
            copy.start()
            sends.append(copy)
    return sends, lambda f: total(f, 0, bits)


def kernel(
    n,
    target,
    links,
    scale,
    loads_hbm,
    operators_hbm,
    basis_hbm,
    coarse_hbm,
    start_ref,
    resid_ref,
    loads,
    operators,
    basis,
    coarse,
    runs,
    gat,
    stage,
    recv,
    cacc,
    cpart,
    cgot,
    call,
    dual,
    in_sem,
    op_sem,
    send_sem,
    recv_sem,
    csend_sem,
    crecv_sem,
    dsend_sem,
    drecv_sem,
    gsend_sem,
    grecv_sem,
):
    bits = n.bit_length() - 1
    me = lax.axis_index("sub")
    subs, columns, rows_in = loads.shape
    per_sub = rows_in // BLK
    nblocks = subs * per_sub
    own_blocks = gat.shape[0] // n
    per = own_blocks // FLOWS

    barrier = pltpu.get_barrier_semaphore()
    for r in range(1, n):
        pl.semaphore_signal(
            barrier, inc=1, device_id={"sub": flip(me, r, bits)}, device_id_type=MESH
        )
    load_copy = pltpu.make_async_copy(loads_hbm, loads, in_sem.at[0])
    basis_copy = pltpu.make_async_copy(basis_hbm, basis, in_sem.at[1])
    coarse_copy = pltpu.make_async_copy(coarse_hbm, coarse, in_sem.at[2])

    def op_copy(s):
        return pltpu.make_async_copy(operators_hbm.at[s], operators.at[s], op_sem.at[s])

    load_copy.start()
    for s in range(subs):
        op_copy(s).start()
    basis_copy.start()
    coarse_copy.start()
    runs[nblocks] = jnp.zeros((columns, BLK), F32)
    weight = 1.0 / (1.0 + scale[...].astype(F32))
    load_copy.wait()

    def add_runs(s, prod):
        for j in range(per_sub):
            row = s * per_sub + j
            term = prod[:, j * BLK : (j + 1) * BLK].astype(BF16).astype(F32)
            runs[row] = term + runs[links[row]]

    def first(s, carry):
        op_copy(s).wait()
        add_runs(s, jnp.dot(loads[s], operators[s], preferred_element_type=F32))
        return carry

    lax.fori_loop(0, subs, first, 0)

    def local(f, owner):
        base = nblocks + owner * own_blocks + f * per
        return jnp.stack([runs[links[base + i]] for i in range(per)])

    pl.semaphore_wait(barrier, n - 1)
    sends, finish = reduce_scatter(n, bits, me, local, stage, recv, send_sem, recv_sem)
    basis_copy.wait()
    coarse_copy.wait()
    for f in range(FLOWS):
        span = slice(f * per * BLK, (f + 1) * per * BLK)
        part = finish(f)
        pieces = []
        for i in range(per):
            blk = f * per + i
            pieces.append(part[i] * weight[blk : blk + 1, :])
        wide = jnp.concatenate(pieces, axis=1)
        dual[:, span] = wide
        coeff = jnp.dot(wide.astype(BF16), basis[span], preferred_element_type=F32)
        if f == 0:
            cacc[...] = coeff
        else:
            cacc[...] += coeff

    groups, width = (call.shape[0], call.shape[2])
    rows = n // groups
    tall = columns // rows

    def piece(ref, p):
        return ref.at[p // rows, pl.ds(pl.multiple_of(p % rows * tall, tall), tall)]

    for c in range(groups):
        cpart[c] = cacc[:, c * width : (c + 1) * width].astype(BF16)
    out = []
    for r in range(1, n):
        peer = flip(me, r, bits)
        copy = pltpu.make_async_remote_copy(
            src_ref=piece(cpart, peer),
            dst_ref=cgot.at[r],
            send_sem=csend_sem.at[r],
            recv_sem=crecv_sem.at[r],
            device_id={"sub": peer},
            device_id_type=MESH,
        )
        copy.start()
        out.append(copy)
    mine = piece(cpart, me)[...].astype(F32)
    for r, copy in zip(range(1, n), out):
        copy.wait_recv()
        mine = mine + cgot[r].astype(F32)
    piece(call, me)[...] = mine.astype(BF16)
    back = []
    for r in range(1, n):
        copy = pltpu.make_async_remote_copy(
            src_ref=piece(call, me),
            dst_ref=piece(call, me),
            send_sem=dsend_sem.at[r],
            recv_sem=drecv_sem.at[r],
            device_id={"sub": flip(me, r, bits)},
            device_id_type=MESH,
        )
        copy.start()
        back.append(copy)
    for r, copy in zip(range(1, n), back):
        there = piece(call, flip(me, r, bits))
        pltpu.make_async_remote_copy(
            src_ref=there,
            dst_ref=there,
            send_sem=dsend_sem.at[r],
            recv_sem=drecv_sem.at[r],
            device_id={"sub": flip(me, r, bits)},
            device_id_type=MESH,
        ).wait_recv()
    solved = jnp.dot(call[0], coarse[0:width], preferred_element_type=F32)
    for c in range(1, groups):
        solved = solved + jnp.dot(
            call[c], coarse[c * width : (c + 1) * width], preferred_element_type=F32
        )
    solved = solved.astype(BF16)
    orders = [order[::-1] for order in plan(bits, FLOWS)]

    def gather_copy(f, r, b):
        where = gat.at[pl.ds(flip(me, r, bits) * own_blocks + f * per, per)]
        land = r ^ (1 << b)
        return pltpu.make_async_remote_copy(
            src_ref=where,
            dst_ref=where,
            send_sem=gsend_sem.at[f, land],
            recv_sem=grecv_sem.at[f, land],
            device_id={"sub": flip(me, 1 << b, bits)},
            device_id_type=MESH,
        )

    def arrived(f, r):
        where = gat.at[pl.ds(flip(me, r, bits) * own_blocks + f * per, per)]
        pltpu.make_async_remote_copy(
            src_ref=where,
            dst_ref=where,
            send_sem=gsend_sem.at[f, r],
            recv_sem=grecv_sem.at[f, r],
            device_id={"sub": flip(me, 1, bits)},
            device_id_type=MESH,
        ).wait_recv()

    gathers = []
    for f in range(FLOWS):
        span = slice(f * per * BLK, (f + 1) * per * BLK)
        part = lax.dot_general(
            solved, basis[span], (((1,), (1,)), ((), ())), preferred_element_type=F32
        )
        start_ref[:, span] = part
        for i in range(per):
            gat[me * own_blocks + f * per + i] = part[:, i * BLK : (i + 1) * BLK].astype(BF16)
        for b in orders[f]:
            copy = gather_copy(f, 0, b)
            copy.start()
            gathers.append(copy)
    known = [[] for _ in range(FLOWS)]
    for u in range(bits):
        for f in range(FLOWS):
            b = orders[f][u]
            if u > 0:
                last = 1 << orders[f][u - 1]
                fresh = [last] + [r ^ last for r in known[f]]
                for r in fresh:
                    arrived(f, r)
                known[f] = known[f] + fresh
                for r in known[f]:
                    copy = gather_copy(f, r, b)
                    copy.start()
                    gathers.append(copy)
    for copy in sends + out + back:
        copy.wait_send()
    for f in range(FLOWS):
        last = 1 << orders[f][bits - 1]
        for r in [last] + [r ^ last for r in known[f]]:
            arrived(f, r)

    def second(s, carry):
        picked = [gat[target[s * per_sub + j]] for j in range(per_sub)]
        held = jnp.concatenate(picked, axis=1)
        add_runs(s, jnp.dot(held, operators[s], preferred_element_type=F32))
        return carry

    lax.fori_loop(0, subs, second, 0)
    sends, finish = reduce_scatter(n, bits, me, local, stage, recv, send_sem, recv_sem)
    for f in range(FLOWS):
        part = finish(f)
        for i in range(per):
            blk = f * per + i
            span = slice(blk * BLK, (blk + 1) * BLK)
            resid_ref[:, span] = dual[:, span] - part[i] * weight[blk : blk + 1, :]
    for copy in gathers + sends:
        copy.wait_send()


def hand_over(start_in, resid_in, start_out, resid_out):
    start_out[...] = start_in[...]
    resid_out[...] = resid_in[...]


def per_device(n, loads, operators, owner, dual_block, scale_index, basis, coarse):
    subs, columns, rows_in = loads.shape
    local_rows = basis.shape[0]
    own_blocks = local_rows // BLK
    duals = n * own_blocks
    target = owner.reshape(-1) * own_blocks + dual_block
    nblocks = target.shape[0]
    key = jnp.concatenate([target, jnp.arange(duals, dtype=jnp.int32)])
    bound = jnp.minimum(jnp.arange(nblocks + duals, dtype=jnp.int32), nblocks)
    places = jnp.arange(nblocks, dtype=jnp.int32)
    hit = (key[:, None] == target[None, :]) & (places[None, :] < bound[:, None])
    found = jnp.max(jnp.where(hit, places[None, :], -1), axis=1)
    links = jnp.where(found < 0, nblocks, found)
    scale = scale_index.reshape(own_blocks, BLK)
    per = own_blocks // FLOWS
    dirs = coarse.shape[0]
    rows = min(n, columns // 16)
    groups = n // rows
    vmem = pl.BlockSpec(memory_space=pltpu.VMEM)
    smem = pl.BlockSpec(memory_space=pltpu.SMEM)
    hbm = pl.BlockSpec(memory_space=pl.ANY)
    dma = pltpu.SemaphoreType.DMA
    out = jax.ShapeDtypeStruct((columns, local_rows), F32)
    results = pl.pallas_call(
        functools.partial(kernel, n),
        out_shape=(out, out),
        in_specs=[smem, smem, vmem] + [hbm] * 4,
        out_specs=(vmem, vmem),
        scratch_shapes=[
            pltpu.VMEM(loads.shape, BF16),
            pltpu.VMEM(operators.shape, BF16),
            pltpu.VMEM(basis.shape, BF16),
            pltpu.VMEM(coarse.shape, BF16),
            pltpu.VMEM((nblocks + 1, columns, BLK), F32),
            pltpu.VMEM((duals, columns, BLK), BF16),
            pltpu.VMEM((FLOWS, n - 1, per, columns, BLK), BF16),
            pltpu.VMEM((FLOWS, n - 1, per, columns, BLK), BF16),
            pltpu.VMEM((columns, dirs), F32),
            pltpu.VMEM((groups, columns, dirs // groups), BF16),
            pltpu.VMEM((n, columns // rows, dirs // groups), BF16),
            pltpu.VMEM((groups, columns, dirs // groups), BF16),
            pltpu.VMEM((columns, local_rows), F32),
            dma((3,)),
            dma((subs,)),
            dma((FLOWS, n - 1)),
            dma((FLOWS, n - 1)),
            dma((n,)),
            dma((n,)),
            dma((n,)),
            dma((n,)),
            dma((FLOWS, n)),
            dma((FLOWS, n)),
        ],
        compiler_params=pltpu.CompilerParams(
            collective_id=0, has_side_effects=True, vmem_limit_bytes=VMEM_LIMIT
        ),
        name="feti",
    )(target, links, scale, loads, operators, basis, coarse)
    tile = pl.BlockSpec((columns // 2, local_rows), lambda i: (i, 0))
    return pl.pallas_call(
        hand_over,
        out_shape=(out, out),
        grid=(2,),
        in_specs=[tile, tile],
        out_specs=(tile, tile),
        name="hand_over",
    )(*results)


def solution(mesh):
    return jax.shard_map(
        functools.partial(per_device, mesh.shape["sub"]),
        mesh=mesh,
        in_specs=(
            P("sub", "rep", None),
            P("sub", None, None),
            P("sub", None),
            P("sub"),
            P("sub"),
            P("sub", None),
            P(),
        ),
        out_specs=(P("rep", "sub"), P("rep", "sub")),
        check_vma=False,
    )
```

profile of v0, /device:TPU:0, one launch (start us, length us, event | category | flops | bytes accessed | tf_op | source)
XLA Modules:
  0.0 66.1 jit_solution(10077355881075852180)
XLA Ops:
  0.6 0.7 %bitcast_add_fusion.target = s32[64]{0:T(128)S(1)} fusion(s32[64]{0:T(128)} %param.10, s32[64,1]{0,1:T(1,128)} %param.9), kind=kLoop, calls=%fused_computation.6 | loop fusion | flops 128 | bytes 768 | tf_op jit(solution)/shard_map/add | solution.py:328
  1.3 0.0 copy-start
  1.3 0.1 pad_add_fusion
  1.4 0.1 select_reduce_fusion
  1.5 0.6 compare_select_fusion.links
  2.1 0.0 copy-done
  2.1 62.0 %feti.1 = (f32[64,2048]{1,0:T(8,128)}, f32[64,2048]{1,0:T(8,128)}) custom-call(s32[64]{0:T(128)} %copy-done, s32[192]{0:T(256)} %compare_select_fusion.links, s32[16,128]{1,0:T(8,128)} %bitcast.3, bf16[8,64,1024]{2,1,0:T(8,128)(2,1)} %loads_hbm.1, bf16[8,1024,1024]{2,1,0:T(8,128)(2,1)} %operators_hbm.1, bf16[2048,1024]{1,0:T(8,128)(2,1)} %basis_hbm.1, ...), custom_call_target="tpu_custom_call" | custom-call | tf_op jit(solution)/shard_map/feti/pallas_call | solution.py:346
  64.0 2.0 %hand_over.1 = (f32[64,2048]{1,0:T(8,128)}, f32[64,2048]{1,0:T(8,128)}) custom-call(f32[64,2048]{1,0:T(8,128)} %get-tuple-element.4.start_in, f32[64,2048]{1,0:T(8,128)} %get-tuple-element.5.resid_in), custom_call_target="tpu_custom_call" | custom-call | tf_op jit(solution)/shard_map/hand_over/pallas_call | solution.py:382
  (1 shorter events, 0.0 us)
Async XLA Ops:
  1.3 0.7 %copy-start = (s32[64]{0:T(128)}, s32[64]{0:T(128)S(1)}, u32[]{:S(2)}) copy-start(s32[64]{0:T(128)S(1)} %bitcast_add_fusion.target) | copy-start | bytes 772
where the time goes:
time: 66.3 us; the launch traced here: 66.1 us
  Pallas kernels  64 us (97%)
  other arithmetic  1.42 us (2%)
    pallas_call x1, Pallas kernels, per_device(): pl.pallas_call(functools.partial(kernel, n), out_shape=(out, out), in_spe...  62 us
    pallas_call x1, Pallas kernels, per_device(): pl.pallas_call(hand_over, out_shape=(out, out), grid=(2,), in_specs=[tile...  2.04 us

commit v1 on v0

v1 whole, which is shorter than its diff:
```python
import functools

import jax
import jax.numpy as jnp
from jax import lax
from jax.experimental import pallas as pl
from jax.experimental.pallas import tpu as pltpu
from jax.sharding import PartitionSpec as P

BLK = 128
LANES = 128
FLOWS = 4
AHEAD = 3
MESH = pl.DeviceIdType.MESH
VMEM_LIMIT = 62 * 1024 * 1024
F32 = jnp.float32
BF16 = jnp.bfloat16
I32 = jnp.int32


def flip(me, r, bits):
    out = me
    for b in range(bits):
        if (r >> b) & 1:
            out = out + (1 - 2 * (me // (1 << b) % 2)) * (1 << b)
    return out


def plan(bits, flows):
    rest = list(range(1, bits))
    return [[0] + (rest if f % 2 == 0 else rest[::-1]) for f in range(flows)]


def step_of(r, order):
    for t, b in enumerate(order):
        if (r >> b) & 1:
            return t
    return len(order)


def slot_table(n, order):
    table, done = {}, 0
    for t, b in enumerate(order):
        done |= 1 << b
        for r in range(n):
            if r & done == 0:
                table[(t, r)] = len(table)
    return table


def remote(src, dst, send_sem, recv_sem, peer):
    return pltpu.make_async_remote_copy(
        src_ref=src,
        dst_ref=dst,
        send_sem=send_sem,
        recv_sem=recv_sem,
        device_id={"sub": peer},
        device_id_type=MESH,
    )


class ReduceScatter:
    def __init__(self, n, bits, me, local, stage, recv, send_sem, recv_sem):
        self.n, self.bits, self.me, self.local = n, bits, me, local
        self.stage, self.recv = stage, recv
        self.send_sem, self.recv_sem = send_sem, recv_sem
        self.orders = plan(bits, FLOWS)
        self.tables = [slot_table(n, order) for order in self.orders]
        self.met = [False] * FLOWS

    def sem_of(self, f, slot):
        return self.recv_sem.at[f, max(0, slot - self.n // 2 + 1)]

    def wait(self, f, r, t):
        slot = self.tables[f][(t, r)]
        where = self.recv.at[f, slot]
        if t == 0:
            if self.met[f]:
                return
            self.met[f] = True
            where = self.recv.at[f, pl.ds(0, self.n // 2)]
        peer = flip(self.me, 1 << self.orders[f][t], self.bits)
        remote(where, where, self.send_sem, self.sem_of(f, slot), peer).wait_recv()

    def total(self, f, r, steps):
        part = self.local(f, flip(self.me, r, self.bits))
        for t in range(steps):
            self.wait(f, r, t)
            part = part + self.recv[f, self.tables[f][(t, r)]].astype(F32)
        return part

    def step(self, t, lands=None):
        group = []
        for f in range(FLOWS):
            for r in range(self.n):
                if step_of(r, self.orders[f]) == t:
                    land = r ^ (1 << self.orders[f][t])
                    when = step_of(land, self.orders[f])
                    if lands is None or when in lands:
                        group.append((f if t == 0 else 0, when, f, r, land))
        for _, _, f, r, land in sorted(group):
            self.stage[f, r - 1] = self.total(f, r, t).astype(BF16)
            slot = self.tables[f][(t, land)]
            peer = flip(self.me, 1 << self.orders[f][t], self.bits)
            remote(
                self.stage.at[f, r - 1],
                self.recv.at[f, slot],
                self.send_sem,
                self.sem_of(f, slot),
                peer,
            ).start()

    def finish(self, f):
        return self.total(f, 0, self.bits)

    def drain(self):
        peer = flip(self.me, 1, self.bits)
        remote(self.stage, self.recv, self.send_sem, self.recv_sem.at[0, 0], peer).wait_send()


class SumToAll:
    def __init__(self, n, bits, me, part, got, every, sems):
        self.n, self.bits, self.me = n, bits, me
        self.part, self.got, self.every, self.sems = part, got, every, sems
        self.groups, self.wide = part.shape[0], part.shape[2]
        self.rows = n // self.groups
        self.tall = part.shape[1] // self.rows

    def piece(self, ref, p):
        start = pl.multiple_of(p % self.rows * self.tall, self.tall)
        return ref.at[p // self.rows, pl.ds(start, self.tall)]

    def whole(self, way):
        where = self.got.at[pl.ds(1, self.n - 1)]
        peer = flip(self.me, 1, self.bits)
        return remote(where, where, self.sems.at[2 * way], self.sems.at[2 * way + 1], peer)

    def spread(self, acc):
        for c in range(self.groups):
            self.part[c] = acc[:, c * self.wide : (c + 1) * self.wide].astype(BF16)
        for r in range(1, self.n):
            peer = flip(self.me, r, self.bits)
            src, dst = self.piece(self.part, peer), self.got.at[r]
            remote(src, dst, self.sems.at[0], self.sems.at[1], peer).start()

    def gather(self):
        mine = self.piece(self.part, self.me)[...].astype(F32)
        self.whole(0).wait_recv()
        for r in range(1, self.n):
            mine = mine + self.got[r].astype(F32)
        where = self.piece(self.every, self.me)
        where[...] = mine.astype(BF16)
        for r in range(1, self.n):
            peer = flip(self.me, r, self.bits)
            remote(where, where, self.sems.at[2], self.sems.at[3], peer).start()

    def arrive(self):
        self.whole(1).wait_recv()

    def drain(self):
        self.whole(0).wait_send()
        self.whole(1).wait_send()


class AllGather:
    def __init__(self, n, bits, me, own_blocks, store, send_sem, recv_sem):
        self.n, self.bits, self.me = n, bits, me
        self.own_blocks, self.per = own_blocks, own_blocks // FLOWS
        self.store, self.send_sem, self.recv_sem = store, send_sem, recv_sem
        self.orders = [order[::-1] for order in plan(bits, FLOWS)]
        self.known = [[0] for _ in range(FLOWS)]

    def copy_of(self, f, r, land, b):
        base = flip(self.me, r, self.bits) * self.own_blocks + f * self.per
        where = self.store.at[pl.ds(base, self.per)]
        sem = self.recv_sem.at[0, 0] if land % 2 else self.recv_sem.at[f, land // 2]
        return remote(where, where, self.send_sem, sem, flip(self.me, 1 << b, self.bits))

    def send(self, f, r, u):
        for b in self.orders[f][u:]:
            self.copy_of(f, r, r ^ (1 << b), b).start()

    def begin(self, f):
        self.send(f, 0, 0)

    def step(self, u):
        for f in range(FLOWS):
            last = 1 << self.orders[f][u - 1]
            fresh = [r ^ last for r in self.known[f]]
            for r in fresh:
                self.copy_of(f, r, r, 1).wait_recv()
                self.send(f, r, u)
            self.known[f] = self.known[f] + fresh

    def whole(self, count):
        where = self.store.at[pl.ds(0, count * self.own_blocks)]
        peer = flip(self.me, 1, self.bits)
        return remote(where, where, self.send_sem, self.recv_sem.at[0, 0], peer)

    def arrive(self):
        self.whole(self.n // 2).wait_recv()

    def drain(self):
        self.whole(self.n - 1).wait_send()


def find_links(owner, block, own_blocks, index, duals):
    nblocks = owner.shape[1]
    target = owner[...] * own_blocks + block[...]
    rows = lax.broadcasted_iota(I32, (nblocks, nblocks), 0)
    cols = lax.broadcasted_iota(I32, (nblocks, nblocks), 1)
    wide = jnp.broadcast_to(target, (nblocks, nblocks))
    down = jnp.max(jnp.where(rows == cols, wide, -1), axis=1, keepdims=True)
    before = jnp.where((down == wide) & (rows < cols), rows, -1)
    before = jnp.max(before, axis=0, keepdims=True)
    names = lax.broadcasted_iota(I32, (nblocks, duals), 1)
    places = lax.broadcasted_iota(I32, (nblocks, duals), 0)
    last = jnp.max(jnp.where(down == names, places, -1), axis=0, keepdims=True)
    index[0:1, 0:nblocks] = target
    index[1:2, 0:nblocks] = jnp.where(before < 0, nblocks, before)
    index[2:3, 0:duals] = jnp.where(last < 0, nblocks, last)


def kernel(
    n,
    owner_ref,
    block_ref,
    scale,
    loads_hbm,
    operators_hbm,
    basis_hbm,
    coarse_hbm,
    start_hbm,
    resid_hbm,
    loads,
    operators,
    basis,
    coarse,
    runs,
    index,
    table,
    stage,
    recv,
    cacc,
    cpart,
    cgot,
    call,
    start_v,
    dual,
    in_sem,
    op_sem,
    load_sem,
    out_sem,
    send_sem,
    recv_sem,
    sum_sem,
    gsend_sem,
    grecv_sem,
    *gat,
):
    bits = n.bit_length() - 1
    me = lax.axis_index("sub")
    subs, columns, rows_in = loads.shape
    per_sub = rows_in // BLK
    nblocks = subs * per_sub
    chunks, (duals, high, _) = len(gat), gat[0].shape
    own_blocks = duals // n
    per = own_blocks // FLOWS
    flows = range(FLOWS)
    target = lambda i: table[0, i]
    before = lambda i: table[1, i]
    last = lambda i: table[2, i]

    barrier = pltpu.get_barrier_semaphore()
    for r in range(1, n):
        pl.semaphore_signal(
            barrier, inc=1, device_id={"sub": flip(me, r, bits)}, device_id_type=MESH
        )
    basis_copy = pltpu.make_async_copy(basis_hbm, basis, in_sem.at[0])
    coarse_copy = pltpu.make_async_copy(coarse_hbm, coarse, in_sem.at[1])
    table_copy = pltpu.make_async_copy(index, table, in_sem.at[2])

    def load_copy(s):
        return pltpu.make_async_copy(loads_hbm.at[s], loads.at[s], load_sem.at[s])

    def op_copy(s):
        return pltpu.make_async_copy(operators_hbm.at[s], operators.at[s], op_sem.at[s])

    ahead = min(AHEAD, subs)
    for s in range(ahead):
        load_copy(s).start()
        op_copy(s).start()
    find_links(owner_ref, block_ref, own_blocks, index, duals)
    table_copy.start()
    runs[nblocks] = jnp.zeros((columns, BLK), F32)
    weight = 1.0 / (1.0 + scale[...].astype(F32))
    table_copy.wait()

    def add_runs(s, span, prod):
        for j in range(per_sub):
            row = s * per_sub + j
            term = prod[:, j * BLK : (j + 1) * BLK].astype(BF16).astype(F32)
            runs[row, span] = term + runs[before(row), span]

    def first(s, carry):
        load_copy(s).wait()
        op_copy(s).wait()

        @pl.when(s + ahead < subs)
        def _():
            load_copy(s + ahead).start()
            op_copy(s + ahead).start()

        @pl.when(s + ahead == subs)
        def _():
            basis_copy.start()
            coarse_copy.start()

        add_runs(s, slice(None), jnp.dot(loads[s], operators[s], preferred_element_type=F32))
        return carry

    lax.fori_loop(0, subs, first, 0)
    pl.semaphore_wait(barrier, n - 1)

    spans = [slice(h * high, (h + 1) * high) for h in range(chunks)]

    def scatter_of(h):
        def local(f, owner):
            base = owner * own_blocks + f * per
            return jnp.stack([runs[last(base + i), spans[h]] for i in range(per)])

        return ReduceScatter(
            n, bits, me, local, stage.at[h], recv.at[h], send_sem.at[h], recv_sem.at[h]
        )

    one = [scatter_of(h) for h in range(chunks)]
    two = [scatter_of(h) for h in range(chunks)]
    sums = [
        SumToAll(
            n, bits, me, cpart.at[h], cgot.at[h], call.at[h], sum_sem.at[h]
        )
        for h in range(chunks)
    ]
    gathers = [
        AllGather(n, bits, me, own_blocks, gat[h], gsend_sem.at[h], grecv_sem.at[h])
        for h in range(chunks)
    ]

    def project(h):
        for f in flows:
            span = slice(f * per * BLK, (f + 1) * per * BLK)
            part = one[h].finish(f)
            pieces = []
            for i in range(per):
                blk = f * per + i
                pieces.append(part[i] * weight[blk : blk + 1, :])
            wide = jnp.concatenate(pieces, axis=1)
            dual[spans[h], span] = wide
            coeff = jnp.dot(wide.astype(BF16), basis[span], preferred_element_type=F32)
            if f == 0:
                cacc[h] = coeff
            else:
                cacc[h] += coeff
        sums[h].spread(cacc.at[h])

    def out_copy(h, which):
        src, dst = ((start_v, start_hbm), (dual, resid_hbm))[which]
        return pltpu.make_async_copy(src.at[spans[h]], dst.at[spans[h]], out_sem.at[h, which])

    def solve(h):
        sums[h].arrive()
        groups, width = call.shape[1], call.shape[3]
        solved = jnp.dot(call[h, 0], coarse[0:width], preferred_element_type=F32)
        for c in range(1, groups):
            solved = solved + jnp.dot(
                call[h, c], coarse[c * width : (c + 1) * width], preferred_element_type=F32
            )
        return solved.astype(BF16)

    def rise(h, solved, part_of):
        for f in part_of:
            span = slice(f * per * BLK, (f + 1) * per * BLK)
            part = lax.dot_general(
                solved, basis[span], (((1,), (1,)), ((), ())), preferred_element_type=F32
            )
            start_v[spans[h], span] = part
            for i in range(per):
                where = me * own_blocks + f * per + i
                gat[h][where] = part[:, i * BLK : (i + 1) * BLK].astype(BF16)
            gathers[h].begin(f)
            if f == FLOWS - 1:
                out_copy(h, 0).start()

    def apply(h, lo, hi):
        def second(s, carry):
            picked = [gat[h][target(s * per_sub + j)] for j in range(per_sub)]
            held = jnp.concatenate(picked, axis=1)
            prod = jnp.dot(held, operators[s], preferred_element_type=F32)
            add_runs(s, spans[h], prod)
            return carry

        lax.fori_loop(lo, hi, second, 0)

    def conclude(h):
        for f in flows:
            part = two[h].finish(f)
            for i in range(per):
                blk = f * per + i
                span = slice(blk * BLK, (blk + 1) * BLK)
                dual[spans[h], span] = (
                    dual[spans[h], span] - part[i] * weight[blk : blk + 1, :]
                )
        out_copy(h, 1).start()

    every = range(chunks)
    half = FLOWS // 2
    cut = [subs // 4, 3 * subs // 8, 7 * subs // 8]
    late, early = (bits,), tuple(range(bits))

    def wrap_up(h):
        one[h].drain()
        sums[h].drain()

    for h in every:
        one[h].step(0)
    basis_copy.wait()
    coarse_copy.wait()
    if chunks == 1:
        for t in range(1, bits):
            one[0].step(t)
        project(0)
        sums[0].gather()
        rise(0, solve(0), flows)
        for u in range(1, bits):
            gathers[0].step(u)
        gathers[0].arrive()
        wrap_up(0)
        apply(0, 0, subs)
        for t in range(bits):
            two[0].step(t)
        conclude(0)
    else:
        one[0].step(1)
        one[1].step(1, early)
        for t in range(2, bits):
            one[0].step(t)
        one[1].step(1, late)
        for t in range(2, bits):
            one[1].step(t)
        project(0)
        project(1)
        sums[0].gather()
        sums[1].gather()
        x0 = solve(0)
        rise(0, x0, flows)
        x1 = solve(1)
        rise(1, x1, flows[:half])
        gathers[0].step(1)
        rise(1, x1, flows[half:])
        for u in range(2, bits):
            gathers[0].step(u)
        wrap_up(0)
        gathers[1].step(1)
        gathers[0].arrive()
        apply(0, 0, cut[0])
        for u in range(2, bits):
            gathers[1].step(u)
        apply(0, cut[0], subs)
        two[0].step(0)
        wrap_up(1)
        gathers[1].arrive()
        apply(1, 0, cut[1])
        two[0].step(1)
        apply(1, cut[1], cut[2])
        for t in range(2, bits):
            two[0].step(t)
        apply(1, cut[2], subs)
        two[1].step(0)
        two[1].step(1)
        conclude(0)
        for t in range(2, bits):
            two[1].step(t)
        conclude(1)

    for h in range(chunks):
        for which in range(2):
            out_copy(h, which).wait()
        gathers[h].drain()
        two[h].drain()


def hand_over(start_in, resid_in, start_out, resid_out):
    start_out[...] = start_in[...]
    resid_out[...] = resid_in[...]


def chunks_of(n, columns, dirs):
    half = columns // 2
    groups = n // min(n, max(1, half // 16))
    return 2 if half % 16 == 0 and dirs // groups >= LANES else 1


def per_device(n, loads, operators, owner, dual_block, scale_index, basis, coarse):
    subs, columns, rows_in = loads.shape
    local_rows = basis.shape[0]
    own_blocks = local_rows // BLK
    duals = n * own_blocks
    nblocks = owner.shape[0]
    scale = scale_index.reshape(own_blocks, BLK)
    per = own_blocks // FLOWS
    dirs = coarse.shape[0]
    chunks = chunks_of(n, columns, dirs)
    high = columns // chunks
    rows = min(n, high // 16)
    groups = n // rows
    entries = max(LANES, duals)
    vmem = pl.BlockSpec(memory_space=pltpu.VMEM)
    hbm = pl.BlockSpec(memory_space=pl.ANY)
    dma = pltpu.SemaphoreType.DMA
    out = jax.ShapeDtypeStruct((columns, local_rows), F32)
    blocks = pltpu.VMEM((chunks, FLOWS, n - 1, per, high, BLK), BF16)
    results = pl.pallas_call(
        functools.partial(kernel, n),
        out_shape=(out, out),
        in_specs=[vmem, vmem, vmem] + [hbm] * 4,
        out_specs=(hbm, hbm),
        scratch_shapes=[
            pltpu.VMEM(loads.shape, BF16),
            pltpu.VMEM(operators.shape, BF16),
            pltpu.VMEM(basis.shape, BF16),
            pltpu.VMEM(coarse.shape, BF16),
            pltpu.VMEM((nblocks + 1, columns, BLK), F32),
            pltpu.VMEM((8, entries), I32),
            pltpu.SMEM((8, entries), I32),
            blocks,
            blocks,
            pltpu.VMEM((chunks, high, dirs), F32),
            pltpu.VMEM((chunks, groups, high, dirs // groups), BF16),
            pltpu.VMEM((chunks, n, high // rows, dirs // groups), BF16),
            pltpu.VMEM((chunks, groups, high, dirs // groups), BF16),
            pltpu.VMEM((columns, local_rows), F32),
            pltpu.VMEM((columns, local_rows), F32),
            dma((3,)),
            dma((subs,)),
            dma((subs,)),
            dma((chunks, 2)),
            dma((chunks,)),
            dma((chunks, FLOWS, n // 2)),
            dma((chunks, 4)),
            dma((chunks,)),
            dma((chunks, FLOWS, n // 2)),
        ]
        + [pltpu.VMEM((duals, high, BLK), BF16)] * chunks,
        compiler_params=pltpu.CompilerParams(
            collective_id=0, has_side_effects=True, vmem_limit_bytes=VMEM_LIMIT
        ),
        name="feti",
    )(
        owner.reshape(1, nblocks),
        dual_block.reshape(1, nblocks),
        scale,
        loads,
        operators,
        basis,
        coarse,
    )
    tile = pl.BlockSpec((columns // 2, local_rows), lambda i: (i, 0))
    return pl.pallas_call(
        hand_over,
        out_shape=(out, out),
        grid=(2,),
        in_specs=[tile, tile],
        out_specs=(tile, tile),
        name="hand_over",
    )(*results)


def solution(mesh):
    return jax.shard_map(
        functools.partial(per_device, mesh.shape["sub"]),
        mesh=mesh,
        in_specs=(
            P("sub", "rep", None),
            P("sub", None, None),
            P("sub", None),
            P("sub"),
            P("sub"),
            P("sub", None),
            P(),
        ),
        out_specs=(P("rep", "sub"), P("rep", "sub")),
        check_vma=False,
    )
```

time: 66.3 us -> 59.9 us (0.903)
  Pallas kernels: 64 us -> 59.1 us
  other arithmetic: 1.42 us -> 0 us
    pallas_call x1, Pallas kernels: 62 us -> 57 us  [per_device(): pl.pallas_call(functools.partial(kernel, n), out_shape=(out, out), in_spe...]
    add x1 -> x0, other arithmetic: 0.68 us -> none  [per_device(): target = owner.reshape(-1) * own_blocks + dual_block]
where the time goes in v1:
time: 59.9 us; the launch traced here: 59.7 us
  Pallas kernels  59.1 us (99%)
  between operations  0.64 us (1%)
    pallas_call x1, Pallas kernels, per_device(): pl.pallas_call(functools.partial(kernel, n), out_shape=(out, out), in_spe...  57 us
    pallas_call x1, Pallas kernels, per_device(): pl.pallas_call(hand_over, out_shape=(out, out), grid=(2,), in_specs=[tile...  2.04 us

profile of v1, /device:TPU:0, one launch (start us, length us, event | category | flops | bytes accessed | tf_op | source)
XLA Modules:
  0.0 59.7 jit_solution(13215695358312419312)
XLA Ops:
  0.6 57.0 %feti.1 = (f32[64,2048]{1,0:T(8,128)}, f32[64,2048]{1,0:T(8,128)}) custom-call(s32[1,64]{1,0:T(1,128)} %bitcast.4, s32[1,64]{1,0:T(1,128)} %bitcast.5, s32[16,128]{1,0:T(8,128)} %bitcast.3, bf16[8,64,1024]{2,1,0:T(8,128)(2,1)} %loads_hbm.1, bf16[8,1024,1024]{2,1,0:T(8,128)(2,1)} %operators_hbm.1, bf16[2048,1024]{1,0:T(8,128)(2,1)} %basis_hbm.1, ...), custom_call_target="tpu_custom_call" | custom-call | tf_op jit(solution)/shard_map/feti/pallas_call | solution.py:522
  57.7 2.0 %hand_over.1 = (f32[64,2048]{1,0:T(8,128)}, f32[64,2048]{1,0:T(8,128)}) custom-call(f32[64,2048]{1,0:T(8,128)} %get-tuple-element.4.start_in, f32[64,2048]{1,0:T(8,128)} %get-tuple-element.5.resid_in), custom_call_target="tpu_custom_call" | custom-call | tf_op jit(solution)/shard_map/hand_over/pallas_call | solution.py:568

commit v2 on v1

--- a/solution.py
+++ b/solution.py
@@ -10,9 +10,11 @@
 BLK = 128
 LANES = 128
 FLOWS = 4
+BY_FLOW = (0,)
+CUTS = (2, 5, 1, 6)
 AHEAD = 3
 MESH = pl.DeviceIdType.MESH
-VMEM_LIMIT = 62 * 1024 * 1024
+VMEM_LIMIT = 55 * 1000 * 1000
 F32 = jnp.float32
 BF16 = jnp.bfloat16
 I32 = jnp.int32
@@ -89,15 +91,14 @@
             part = part + self.recv[f, self.tables[f][(t, r)]].astype(F32)
         return part
 
-    def step(self, t, lands=None):
+    def step(self, t, flows=range(FLOWS)):
         group = []
-        for f in range(FLOWS):
+        for f in flows:
             for r in range(self.n):
                 if step_of(r, self.orders[f]) == t:
                     land = r ^ (1 << self.orders[f][t])
                     when = step_of(land, self.orders[f])
-                    if lands is None or when in lands:
-                        group.append((f if t == 0 else 0, when, f, r, land))
+                    group.append((f if t in BY_FLOW else 0, when, f, r, land))
         for _, _, f, r, land in sorted(group):
             self.stage[f, r - 1] = self.total(f, r, t).astype(BF16)
             slot = self.tables[f][(t, land)]
@@ -183,8 +184,8 @@
     def begin(self, f):
         self.send(f, 0, 0)
 
-    def step(self, u):
-        for f in range(FLOWS):
+    def step(self, u, flows=range(FLOWS)):
+        for f in flows:
             last = 1 << self.orders[f][u - 1]
             fresh = [r ^ last for r in self.known[f]]
             for r in fresh:
@@ -204,9 +205,8 @@
         self.whole(self.n - 1).wait_send()
 
 
-def find_links(owner, block, own_blocks, index, duals):
-    nblocks = owner.shape[1]
-    target = owner[...] * own_blocks + block[...]
+def find_links(target, index, duals):
+    nblocks = target.shape[1]
     rows = lax.broadcasted_iota(I32, (nblocks, nblocks), 0)
     cols = lax.broadcasted_iota(I32, (nblocks, nblocks), 1)
     wide = jnp.broadcast_to(target, (nblocks, nblocks))
@@ -223,9 +223,7 @@
 
 def kernel(
     n,
-    owner_ref,
-    block_ref,
-    scale,
+    meta,
     loads_hbm,
     operators_hbm,
     basis_hbm,
@@ -267,9 +265,16 @@
     own_blocks = duals // n
     per = own_blocks // FLOWS
     flows = range(FLOWS)
-    target = lambda i: table[0, i]
-    before = lambda i: table[1, i]
-    last = lambda i: table[2, i]
+
+    def target_of(i):
+        return table[0, i]
+
+    def before(i):
+        return table[1, i]
+
+    def last(i):
+        return table[2, i]
+
 
     barrier = pltpu.get_barrier_semaphore()
     for r in range(1, n):
@@ -290,10 +295,13 @@
     for s in range(ahead):
         load_copy(s).start()
         op_copy(s).start()
-    find_links(owner_ref, block_ref, own_blocks, index, duals)
+    head = meta.shape[0] - own_blocks
+    names = jnp.concatenate([meta[i : i + 1] for i in range(head)], axis=1)
+    target = names[:, :nblocks] * own_blocks + names[:, nblocks : 2 * nblocks]
+    find_links(target, index, duals)
     table_copy.start()
     runs[nblocks] = jnp.zeros((columns, BLK), F32)
-    weight = 1.0 / (1.0 + scale[...].astype(F32))
+    weight = 1.0 / (1.0 + meta[head:].astype(F32))
     table_copy.wait()
 
     def add_runs(s, span, prod):
@@ -347,6 +355,8 @@
     ]
 
     def project(h):
+        if h == 0:
+            basis_copy.wait()
         for f in flows:
             span = slice(f * per * BLK, (f + 1) * per * BLK)
             part = one[h].finish(f)
@@ -368,6 +378,8 @@
         return pltpu.make_async_copy(src.at[spans[h]], dst.at[spans[h]], out_sem.at[h, which])
 
     def solve(h):
+        if h == 0:
+            coarse_copy.wait()
         sums[h].arrive()
         groups, width = call.shape[1], call.shape[3]
         solved = jnp.dot(call[h, 0], coarse[0:width], preferred_element_type=F32)
@@ -393,7 +405,7 @@
 
     def apply(h, lo, hi):
         def second(s, carry):
-            picked = [gat[h][target(s * per_sub + j)] for j in range(per_sub)]
+            picked = [gat[h][target_of(s * per_sub + j)] for j in range(per_sub)]
             held = jnp.concatenate(picked, axis=1)
             prod = jnp.dot(held, operators[s], preferred_element_type=F32)
             add_runs(s, spans[h], prod)
@@ -401,8 +413,8 @@
 
         lax.fori_loop(lo, hi, second, 0)
 
-    def conclude(h):
-        for f in flows:
+    def conclude(h, some=range(FLOWS)):
+        for f in some:
             part = two[h].finish(f)
             for i in range(per):
                 blk = f * per + i
@@ -410,12 +422,12 @@
                 dual[spans[h], span] = (
                     dual[spans[h], span] - part[i] * weight[blk : blk + 1, :]
                 )
-        out_copy(h, 1).start()
+        if some[-1] == FLOWS - 1:
+            out_copy(h, 1).start()
 
     every = range(chunks)
     half = FLOWS // 2
-    cut = [subs // 4, 3 * subs // 8, 7 * subs // 8]
-    late, early = (bits,), tuple(range(bits))
+    cut = [subs * i // 8 for i in CUTS]
 
     def wrap_up(h):
         one[h].drain()
@@ -423,8 +435,6 @@
 
     for h in every:
         one[h].step(0)
-    basis_copy.wait()
-    coarse_copy.wait()
     if chunks == 1:
         for t in range(1, bits):
             one[0].step(t)
@@ -440,46 +450,48 @@
             two[0].step(t)
         conclude(0)
     else:
-        one[0].step(1)
-        one[1].step(1, early)
-        for t in range(2, bits):
+        for t in range(1, bits):
             one[0].step(t)
-        one[1].step(1, late)
+        one[1].step(1)
+        project(0)
         for t in range(2, bits):
             one[1].step(t)
-        project(0)
+        sums[0].gather()
         project(1)
-        sums[0].gather()
+        x0 = solve(0)
+        rise(0, x0, flows[:half])
         sums[1].gather()
-        x0 = solve(0)
-        rise(0, x0, flows)
+        rise(0, x0, flows[half:])
+        gathers[0].step(1, flows[:-1])
         x1 = solve(1)
+        gathers[0].step(1, flows[-1:])
         rise(1, x1, flows[:half])
-        gathers[0].step(1)
-        rise(1, x1, flows[half:])
-        for u in range(2, bits):
-            gathers[0].step(u)
+        for f in flows[half:]:
+            gathers[0].step(2, [f - half])
+            rise(1, x1, [f])
+        gathers[0].step(2, flows[half:])
         wrap_up(0)
-        gathers[1].step(1)
+        gathers[1].step(1, flows[:1])
         gathers[0].arrive()
         apply(0, 0, cut[0])
-        for u in range(2, bits):
-            gathers[1].step(u)
-        apply(0, cut[0], subs)
+        gathers[1].step(1, flows[1:])
+        apply(0, cut[0], cut[1])
+        gathers[1].step(2, flows[:half])
+        apply(0, cut[1], subs)
+        gathers[1].step(2, flows[half:])
         two[0].step(0)
         wrap_up(1)
         gathers[1].arrive()
-        apply(1, 0, cut[1])
+        apply(1, 0, cut[2])
         two[0].step(1)
-        apply(1, cut[1], cut[2])
-        for t in range(2, bits):
-            two[0].step(t)
-        apply(1, cut[2], subs)
+        apply(1, cut[2], cut[3])
+        two[0].step(2, flows[:half])
+        apply(1, cut[3], subs)
         two[1].step(0)
+        two[0].step(2, flows[half:])
         two[1].step(1)
         conclude(0)
-        for t in range(2, bits):
-            two[1].step(t)
+        two[1].step(2)
         conclude(1)
 
     for h in range(chunks):
@@ -489,9 +501,15 @@
         two[h].drain()
 
 
-def hand_over(start_in, resid_in, start_out, resid_out):
-    start_out[...] = start_in[...]
-    resid_out[...] = resid_in[...]
+def hand_over(start_in, resid_in, start_out, resid_out, sem):
+    copies = [
+        pltpu.make_async_copy(start_in, start_out, sem.at[0]),
+        pltpu.make_async_copy(resid_in, resid_out, sem.at[1]),
+    ]
+    for copy in copies:
+        copy.start()
+    for copy in copies:
+        copy.wait()
 
 
 def chunks_of(n, columns, dirs):
@@ -506,7 +524,9 @@
     own_blocks = local_rows // BLK
     duals = n * own_blocks
     nblocks = owner.shape[0]
-    scale = scale_index.reshape(own_blocks, BLK)
+    spare = jnp.zeros((-2 * nblocks % LANES,), I32)
+    meta = jnp.concatenate([owner.reshape(-1), dual_block, spare, scale_index])
+    meta = meta.reshape(-1, LANES)
     per = own_blocks // FLOWS
     dirs = coarse.shape[0]
     chunks = chunks_of(n, columns, dirs)
@@ -522,7 +542,7 @@
     results = pl.pallas_call(
         functools.partial(kernel, n),
         out_shape=(out, out),
-        in_specs=[vmem, vmem, vmem] + [hbm] * 4,
+        in_specs=[vmem] + [hbm] * 4,
         out_specs=(hbm, hbm),
         scratch_shapes=[
             pltpu.VMEM(loads.shape, BF16),
@@ -556,21 +576,19 @@
         ),
         name="feti",
     )(
-        owner.reshape(1, nblocks),
-        dual_block.reshape(1, nblocks),
-        scale,
+        meta,
         loads,
         operators,
         basis,
         coarse,
     )
-    tile = pl.BlockSpec((columns // 2, local_rows), lambda i: (i, 0))
     return pl.pallas_call(
         hand_over,
         out_shape=(out, out),
-        grid=(2,),
-        in_specs=[tile, tile],
-        out_specs=(tile, tile),
+        in_specs=[vmem, vmem],
+        out_specs=(hbm, hbm),
+        scratch_shapes=[dma((2,))],
+        compiler_params=pltpu.CompilerParams(vmem_limit_bytes=4 * out.size * 4),
         name="hand_over",
     )(*results)
 

time: 59.9 us -> 57.8 us (0.965)
  Pallas kernels: 59.1 us -> 56.2 us
  local copies, waits for them, and re-layouts: 0 us -> 0.8 us
    pallas_call x1, Pallas kernels: 57 us -> 55.2 us  [per_device(): pl.pallas_call(functools.partial(kernel, n), out_shape=(out, out), in_spe...]
    pallas_call x1, Pallas kernels: 2.04 us -> 0.99 us  [per_device(): pl.pallas_call(hand_over, out_shape=(out, out), in_specs=[vmem, vmem], ou...]
    concatenate x0 -> x1, local copies, waits for them, and re-layouts: none -> 0.8 us  [per_device(): meta = jnp.concatenate([owner.reshape(-1), dual_block, spare, scale_index])]
where the time goes in v2:
time: 57.8 us; the launch traced here: 57.6 us
  Pallas kernels  56.2 us (97%)
  local copies, waits for them, and re-layouts  0.8 us (1%)
  between operations  0.64 us (1%)
    pallas_call x1, Pallas kernels, per_device(): pl.pallas_call(functools.partial(kernel, n), out_shape=(out, out), in_spe...  55.2 us

profile of v2, /device:TPU:0, one launch (start us, length us, event | category | flops | bytes accessed | tf_op | source)
XLA Modules:
  0.0 57.6 jit_solution(11609529484687650461)
XLA Ops:
  0.6 0.8 %concatenate.3 = s32[2176]{0:T(1024)S(1)} concatenate(s32[64]{0:T(128)} %bitcast.3, s32[64]{0:T(128)} %param.10, s32[2048]{0:T(1024)} %param.11), dimensions={0} | concatenate | bytes 17408 | tf_op jit(solution)/shard_map/concatenate | solution.py:528
  1.4 55.2 %feti.1 = (f32[64,2048]{1,0:T(8,128)S(1)}, f32[64,2048]{1,0:T(8,128)S(1)}) custom-call(s32[17,128]{1,0:T(8,128)S(1)} %bitcast.2, bf16[8,64,1024]{2,1,0:T(8,128)(2,1)} %loads_hbm.1, bf16[8,1024,1024]{2,1,0:T(8,128)(2,1)} %operators_hbm.1, bf16[2048,1024]{1,0:T(8,128)(2,1)} %basis_hbm.1, bf16[1024,1024]{1,0:T(8,128)(2,1)} %coarse_hbm.1), custom_call_target="tpu_custom_call" | custom-call | tf_op jit(solution)/shard_map/feti/pallas_call | solution.py:542
  56.6 1.0 %hand_over.1 = (f32[64,2048]{1,0:T(8,128)}, f32[64,2048]{1,0:T(8,128)}) custom-call(f32[64,2048]{1,0:T(8,128)S(1)} %get-tuple-element.4.start_in, f32[64,2048]{1,0:T(8,128)S(1)} %get-tuple-element.5.resid_in), custom_call_target="tpu_custom_call" | custom-call | tf_op jit(solution)/shard_map/hand_over/pallas_call | solution.py:585

commit v3 on v2

--- a/solution.py
+++ b/solution.py
@@ -11,7 +11,7 @@
 LANES = 128
 FLOWS = 4
 BY_FLOW = (0,)
-CUTS = (2, 5, 1, 6)
+CUTS = (2, 5, 2, 8)
 AHEAD = 3
 MESH = pl.DeviceIdType.MESH
 VMEM_LIMIT = 55 * 1000 * 1000
@@ -228,8 +228,8 @@
     operators_hbm,
     basis_hbm,
     coarse_hbm,
-    start_hbm,
-    resid_hbm,
+    start_ref,
+    resid_ref,
     loads,
     operators,
     basis,
@@ -243,12 +243,10 @@
     cpart,
     cgot,
     call,
-    start_v,
     dual,
     in_sem,
     op_sem,
     load_sem,
-    out_sem,
     send_sem,
     recv_sem,
     sum_sem,
@@ -373,10 +371,6 @@
                 cacc[h] += coeff
         sums[h].spread(cacc.at[h])
 
-    def out_copy(h, which):
-        src, dst = ((start_v, start_hbm), (dual, resid_hbm))[which]
-        return pltpu.make_async_copy(src.at[spans[h]], dst.at[spans[h]], out_sem.at[h, which])
-
     def solve(h):
         if h == 0:
             coarse_copy.wait()
@@ -395,13 +389,11 @@
             part = lax.dot_general(
                 solved, basis[span], (((1,), (1,)), ((), ())), preferred_element_type=F32
             )
-            start_v[spans[h], span] = part
+            start_ref[spans[h], span] = part
             for i in range(per):
                 where = me * own_blocks + f * per + i
                 gat[h][where] = part[:, i * BLK : (i + 1) * BLK].astype(BF16)
             gathers[h].begin(f)
-            if f == FLOWS - 1:
-                out_copy(h, 0).start()
 
     def apply(h, lo, hi):
         def second(s, carry):
@@ -413,17 +405,15 @@
 
         lax.fori_loop(lo, hi, second, 0)
 
-    def conclude(h, some=range(FLOWS)):
-        for f in some:
+    def conclude(h):
+        for f in flows:
             part = two[h].finish(f)
             for i in range(per):
                 blk = f * per + i
                 span = slice(blk * BLK, (blk + 1) * BLK)
-                dual[spans[h], span] = (
+                resid_ref[spans[h], span] = (
                     dual[spans[h], span] - part[i] * weight[blk : blk + 1, :]
                 )
-        if some[-1] == FLOWS - 1:
-            out_copy(h, 1).start()
 
     every = range(chunks)
     half = FLOWS // 2
@@ -462,19 +452,16 @@
         rise(0, x0, flows[:half])
         sums[1].gather()
         rise(0, x0, flows[half:])
-        gathers[0].step(1, flows[:-1])
+        gathers[0].step(1)
         x1 = solve(1)
-        gathers[0].step(1, flows[-1:])
         rise(1, x1, flows[:half])
-        for f in flows[half:]:
-            gathers[0].step(2, [f - half])
-            rise(1, x1, [f])
+        gathers[0].step(2, flows[:half])
+        rise(1, x1, flows[half:])
         gathers[0].step(2, flows[half:])
         wrap_up(0)
-        gathers[1].step(1, flows[:1])
         gathers[0].arrive()
         apply(0, 0, cut[0])
-        gathers[1].step(1, flows[1:])
+        gathers[1].step(1)
         apply(0, cut[0], cut[1])
         gathers[1].step(2, flows[:half])
         apply(0, cut[1], subs)
@@ -495,8 +482,6 @@
         conclude(1)
 
     for h in range(chunks):
-        for which in range(2):
-            out_copy(h, which).wait()
         gathers[h].drain()
         two[h].drain()
 
@@ -543,7 +528,7 @@
         functools.partial(kernel, n),
         out_shape=(out, out),
         in_specs=[vmem] + [hbm] * 4,
-        out_specs=(hbm, hbm),
+        out_specs=(vmem, vmem),
         scratch_shapes=[
             pltpu.VMEM(loads.shape, BF16),
             pltpu.VMEM(operators.shape, BF16),
@@ -559,11 +544,9 @@
             pltpu.VMEM((chunks, n, high // rows, dirs // groups), BF16),
             pltpu.VMEM((chunks, groups, high, dirs // groups), BF16),
             pltpu.VMEM((columns, local_rows), F32),
-            pltpu.VMEM((columns, local_rows), F32),
             dma((3,)),
             dma((subs,)),
             dma((subs,)),
-            dma((chunks, 2)),
             dma((chunks,)),
             dma((chunks, FLOWS, n // 2)),
             dma((chunks, 4)),

time: 57.8 us -> 57 us (0.986)
  Pallas kernels: 56.2 us -> 55.4 us
    pallas_call x1, Pallas kernels: 55.2 us -> 54.4 us  [per_device(): pl.pallas_call(functools.partial(kernel, n), out_shape=(out, out), in_spe...]
where the time goes in v3:
time: 57 us; the launch traced here: 56.8 us
  Pallas kernels  55.4 us (97%)
  local copies, waits for them, and re-layouts  0.8 us (1%)
  between operations  0.64 us (1%)
    pallas_call x1, Pallas kernels, per_device(): pl.pallas_call(functools.partial(kernel, n), out_shape=(out, out), in_spe...  54.4 us

profile of v3, /device:TPU:0, one launch (start us, length us, event | category | flops | bytes accessed | tf_op | source)
XLA Modules:
  0.0 56.8 jit_solution(7837061403473536874)
XLA Ops:
  0.6 0.8 %concatenate.3 = s32[2176]{0:T(1024)S(1)} concatenate(s32[64]{0:T(128)} %bitcast.3, s32[64]{0:T(128)} %param.10, s32[2048]{0:T(1024)} %param.11), dimensions={0} | concatenate | bytes 17408 | tf_op jit(solution)/shard_map/concatenate | solution.py:513
  1.4 54.4 %feti.1 = (f32[64,2048]{1,0:T(8,128)S(1)}, f32[64,2048]{1,0:T(8,128)S(1)}) custom-call(s32[17,128]{1,0:T(8,128)S(1)} %bitcast.2, bf16[8,64,1024]{2,1,0:T(8,128)(2,1)} %loads_hbm.1, bf16[8,1024,1024]{2,1,0:T(8,128)(2,1)} %operators_hbm.1, bf16[2048,1024]{1,0:T(8,128)(2,1)} %basis_hbm.1, bf16[1024,1024]{1,0:T(8,128)(2,1)} %coarse_hbm.1), custom_call_target="tpu_custom_call" | custom-call | tf_op jit(solution)/shard_map/feti/pallas_call | solution.py:527
  55.8 1.0 %hand_over.1 = (f32[64,2048]{1,0:T(8,128)}, f32[64,2048]{1,0:T(8,128)}) custom-call(f32[64,2048]{1,0:T(8,128)S(1)} %get-tuple-element.4.start_in, f32[64,2048]{1,0:T(8,128)S(1)} %get-tuple-element.5.resid_in), custom_call_target="tpu_custom_call" | custom-call | tf_op jit(solution)/shard_map/hand_over/pallas_call | solution.py:568

commit v4 on v3

--- a/solution.py
+++ b/solution.py
@@ -11,7 +11,7 @@
 LANES = 128
 FLOWS = 4
 BY_FLOW = (0,)
-CUTS = (2, 5, 2, 8)
+CUTS = (2, 5, 2)
 AHEAD = 3
 MESH = pl.DeviceIdType.MESH
 VMEM_LIMIT = 55 * 1000 * 1000
@@ -139,7 +139,7 @@
     def spread(self, acc):
         for c in range(self.groups):
             self.part[c] = acc[:, c * self.wide : (c + 1) * self.wide].astype(BF16)
-        for r in range(1, self.n):
+        for r in reversed(range(1, self.n)):
             peer = flip(self.me, r, self.bits)
             src, dst = self.piece(self.part, peer), self.got.at[r]
             remote(src, dst, self.sems.at[0], self.sems.at[1], peer).start()
@@ -151,7 +151,7 @@
             mine = mine + self.got[r].astype(F32)
         where = self.piece(self.every, self.me)
         where[...] = mine.astype(BF16)
-        for r in range(1, self.n):
+        for r in reversed(range(1, self.n)):
             peer = flip(self.me, r, self.bits)
             remote(where, where, self.sems.at[2], self.sems.at[3], peer).start()
 
@@ -471,11 +471,9 @@
         gathers[1].arrive()
         apply(1, 0, cut[2])
         two[0].step(1)
-        apply(1, cut[2], cut[3])
-        two[0].step(2, flows[:half])
-        apply(1, cut[3], subs)
+        apply(1, cut[2], subs)
+        two[0].step(2)
         two[1].step(0)
-        two[0].step(2, flows[half:])
         two[1].step(1)
         conclude(0)
         two[1].step(2)

time: 57 us -> 56.6 us (level)
  no operation moved by 1% of the time
where the time goes in v4:
time: 56.6 us; the launch traced here: 56.4 us
  Pallas kernels  55 us (97%)
  local copies, waits for them, and re-layouts  0.8 us (1%)
  between operations  0.64 us (1%)
    pallas_call x1, Pallas kernels, per_device(): pl.pallas_call(functools.partial(kernel, n), out_shape=(out, out), in_spe...  54 us

profile of v4, /device:TPU:0, one launch (start us, length us, event | category | flops | bytes accessed | tf_op | source)
XLA Modules:
  0.0 56.4 jit_solution(13736140563357822043)
XLA Ops:
  0.6 0.8 %concatenate.3 = s32[2176]{0:T(1024)S(1)} concatenate(s32[64]{0:T(128)} %bitcast.3, s32[64]{0:T(128)} %param.10, s32[2048]{0:T(1024)} %param.11), dimensions={0} | concatenate | bytes 17408 | tf_op jit(solution)/shard_map/concatenate | solution.py:511
  1.4 54.0 %feti.1 = (f32[64,2048]{1,0:T(8,128)S(1)}, f32[64,2048]{1,0:T(8,128)S(1)}) custom-call(s32[17,128]{1,0:T(8,128)S(1)} %bitcast.2, bf16[8,64,1024]{2,1,0:T(8,128)(2,1)} %loads_hbm.1, bf16[8,1024,1024]{2,1,0:T(8,128)(2,1)} %operators_hbm.1, bf16[2048,1024]{1,0:T(8,128)(2,1)} %basis_hbm.1, bf16[1024,1024]{1,0:T(8,128)(2,1)} %coarse_hbm.1), custom_call_target="tpu_custom_call" | custom-call | tf_op jit(solution)/shard_map/feti/pallas_call | solution.py:525
  55.4 1.0 %hand_over.1 = (f32[64,2048]{1,0:T(8,128)}, f32[64,2048]{1,0:T(8,128)}) custom-call(f32[64,2048]{1,0:T(8,128)S(1)} %get-tuple-element.4.start_in, f32[64,2048]{1,0:T(8,128)S(1)} %get-tuple-element.5.resid_in), custom_call_target="tpu_custom_call" | custom-call | tf_op jit(solution)/shard_map/hand_over/pallas_call | solution.py:566

commit v5 on v4

--- a/solution.py
+++ b/solution.py
@@ -12,7 +12,7 @@
 FLOWS = 4
 BY_FLOW = (0,)
 CUTS = (2, 5, 2)
-AHEAD = 3
+AHEAD = 4
 MESH = pl.DeviceIdType.MESH
 VMEM_LIMIT = 55 * 1000 * 1000
 F32 = jnp.float32

time: 56.6 us -> 56.6 us (level)
  no operation moved by 1% of the time
where the time goes in v5:
time: 56.6 us; the launch traced here: 56.3 us
  Pallas kernels  54.9 us (97%)
  local copies, waits for them, and re-layouts  0.8 us (1%)
  between operations  0.64 us (1%)
    pallas_call x1, Pallas kernels, per_device(): pl.pallas_call(functools.partial(kernel, n), out_shape=(out, out), in_spe...  53.9 us

profile of v5, /device:TPU:0, one launch (start us, length us, event | category | flops | bytes accessed | tf_op | source)
XLA Modules:
  0.0 56.3 jit_solution(16502214099829235082)
XLA Ops:
  0.6 0.8 %concatenate.3 = s32[2176]{0:T(1024)S(1)} concatenate(s32[64]{0:T(128)} %bitcast.3, s32[64]{0:T(128)} %param.10, s32[2048]{0:T(1024)} %param.11), dimensions={0} | concatenate | bytes 17408 | tf_op jit(solution)/shard_map/concatenate | solution.py:511
  1.4 53.9 %feti.1 = (f32[64,2048]{1,0:T(8,128)S(1)}, f32[64,2048]{1,0:T(8,128)S(1)}) custom-call(s32[17,128]{1,0:T(8,128)S(1)} %bitcast.2, bf16[8,64,1024]{2,1,0:T(8,128)(2,1)} %loads_hbm.1, bf16[8,1024,1024]{2,1,0:T(8,128)(2,1)} %operators_hbm.1, bf16[2048,1024]{1,0:T(8,128)(2,1)} %basis_hbm.1, bf16[1024,1024]{1,0:T(8,128)(2,1)} %coarse_hbm.1), custom_call_target="tpu_custom_call" | custom-call | tf_op jit(solution)/shard_map/feti/pallas_call | solution.py:525
  55.4 1.0 %hand_over.1 = (f32[64,2048]{1,0:T(8,128)}, f32[64,2048]{1,0:T(8,128)}) custom-call(f32[64,2048]{1,0:T(8,128)S(1)} %get-tuple-element.4.start_in, f32[64,2048]{1,0:T(8,128)S(1)} %get-tuple-element.5.resid_in), custom_call_target="tpu_custom_call" | custom-call | tf_op jit(solution)/shard_map/hand_over/pallas_call | solution.py:566
